TPU v7x, 512 devices: a whole 4x8x8 slice. The times are simulated.
512 devices in a mesh: row: 64 (over x, y, z_hi), col: 8 (over z_lo, core).
Axes of the slice: x: 4, y: 8, z: 8 (z_hi: 2, z_lo: 4; z = z_hi * 4 + z_lo), core: 2. Of those that a mesh axis runs over, the one named last changes fastest.
Arguments:
- features: float32 [16384, 512], P('row', 'col'), may hold values from -20 to 20
- adj_values: bfloat16 [256, 64, 4096], P('row', 'col'), may hold values from 0 to 0.0078125
- adj_cols: int32 [256, 64], P('row', 'col'), may hold values from 0 to 255, as said below
- adj_count: int32 [256], P('row'), may hold values from 16 to 64, as said below
Outputs:
- hop_one: float32 [16384, 512], P('row', 'col')
- hop_two: float32 [16384, 512], P('row', 'col')
Inputs may be any that keep to these rules, and one draw needn't show every extreme that they name: `adj_cols`: within one row block the column blocks of all 64 slots are distinct. `adj_count`: some row block has all 64 slots live.
All inputs are finite; a program needn't handle non-finite values.
Results may differ from a plain program's by a relative error of at most 0.0003.
Values may be sent and summed in bfloat16 or wider, within the bound.
A program may use at most 128 MiB of HBM per device.

v0:
```python
import jax
import jax.numpy as jnp
from jax import lax
from jax.sharding import PartitionSpec as P

BLK = 64


def masked_tiles(tile_all, adj_count):
    slot_total = tile_all.shape[1]
    slot_ids = jnp.arange(slot_total, dtype=jnp.int32)
    live_mask = (slot_ids[None, :] < adj_count[:, None]).astype(jnp.float32)
    weights = tile_all.astype(jnp.float32).reshape(tile_all.shape[0], slot_total, BLK, BLK)
    return weights * live_mask[:, :, None, None]


def propagate(slab, weights, col_all):
    feat_width = slab.shape[1]
    blocks = slab.reshape(-1, BLK, feat_width)

    def single(record):
        weight_set, col_ids = record
        picked = blocks[col_ids]
        return jnp.einsum("kij,kjf->if", weight_set, picked, precision=lax.Precision.HIGHEST)

    result = lax.map(single, (weights, col_all))
    return result.reshape(-1, feat_width)


def local(features, adj_values, adj_cols, adj_count):
    tile_all, col_all = (
        lax.all_gather(adj_values, "col", axis=1, tiled=True),
        lax.all_gather(adj_cols, "col", axis=1, tiled=True),
    )
    weights = masked_tiles(tile_all, adj_count)
    slab = lax.all_gather(features, "row", axis=0, tiled=True)
    hop_one = propagate(slab, weights, col_all)
    second_slab = lax.all_gather(hop_one, "row", axis=0, tiled=True)
    hop_two = propagate(second_slab, weights, col_all)
    return (hop_one, hop_two)


def solution(mesh):
    in_specs = (P("row", "col"), P("row", "col", None), P("row", "col"), P("row"))
    out_specs = (P("row", "col"), P("row", "col"))
    return jax.shard_map(local, mesh=mesh, in_specs=in_specs, out_specs=out_specs, check_vma=False)
```

profile of v0, /device:TPU:2, one launch (start us, length us, event | category | flops | bytes accessed | tf_op | source)
XLA Modules:
  0.0 467.1 jit_solution(14740028736777230822)
XLA Ops:
  7.2 0.0 all-gather.5.cloned.1.call-start
  7.2 0.7 all-gather.5.cloned.1.call-update
  7.9 0.0 all-gather.7.cloned.1.call-start
  7.9 0.7 all-gather.7.cloned.1.call-update
  8.6 0.0 all-gather.9.cloned.1.call-start
  8.7 15.2 %all-gather = s32[8,8,4]{1,2,0:T(4,128)S(1)} all-gather(s32[1,8,4]{1,2,0:T(4,128)} %bitcast.70), channel_id=1, replica_groups=mesh['row'=64,'col'=8] {'col'}, dimensions={0}, use_global_device_ids=true | all-gather | bytes 1152 | tf_op jit(solution)/shard_map/all_gather | solution.py:33
  23.9 0.1 reshape.125
  23.9 0.7 fusion.34
  24.7 31.9 %all-gather.5.cloned.1.call-done = bf16[4,64,4096]{2,1,0:T(8,128)(2,1)} async-done(((bf16[4,8,4096]{2,1,0:T(8,128)(2,1)}), bf16[4,64,4096]{2,1,0:T(8,128)(2,1)}) %all-gather.5.cloned.1.call-update) | async-done | bytes 2097168 | tf_op jit(solution)/shard_map/all_gather | solution.py:32
  56.6 7.0 %reshape.107 = f32[4,64,64,64]{3,2,1,0:T(8,128)} reshape(bf16[4,64,4096]{2,1,0:T(8,128)(2,1)} %all-gather.5.cloned.1.call-done) | data formatting | bytes 6291456 | tf_op jit(solution)/shard_map/reshape | solution.py:13
  63.6 7.2 %broadcast_multiply_fusion = f32[4,64,64,64]{3,2,1,0:T(8,128)} fusion(f32[4,64,64,64]{3,2,1,0:T(8,128)} %reshape.107, f32[4,64]{1,0:T(4,128)S(1)} %fusion.34), kind=kLoop, calls=%fused_computation.26 | loop fusion | flops 1048576 | bytes 8389632 | tf_op jit(solution)/shard_map/mul | solution.py:14
  70.8 9.0 %copy.25 = f32[4,64,64,64]{1,2,3,0:T(8,128)} copy(f32[4,64,64,64]{3,2,1,0:T(8,128)} %broadcast_multiply_fusion) | data formatting | bytes 8388608 | tf_op jit(solution)/shard_map/while | solution.py:26
  79.8 141.0 %all-gather.7.cloned.1.call-done = f32[16384,64]{0,1:T(8,128)} async-done(((f32[256,64]{0,1:T(8,128)}), f32[16384,64]{0,1:T(8,128)}) %all-gather.7.cloned.1.call-update) | async-done | bytes 4194320 | tf_op jit(solution)/shard_map/all_gather | solution.py:36
  220.8 6.9 %copy.24 = f32[16384,64]{1,0:T(8,128)} copy(f32[16384,64]{0,1:T(8,128)} %all-gather.7.cloned.1.call-done) | data formatting | bytes 8388608 | tf_op jit(solution)/shard_map/all_gather | solution.py:36
  227.7 35.2 %while.20 = (s32[]{:T(128)}, f32[4,64,64]{2,1,0:T(8,128)S(1)}, f32[4,64,64,64]{1,2,3,0:T(8,128)}, s32[4,64]{1,0:T(4,128)S(1)}, f32[256,64,64]{2,1,0:T(8,128)}, /*index=5*/s32[]{:T(128)}) while((s32[]{:T(128)}, f32[4,64,64]{2,1,0:T(8,128)S(1)}, f32[4,64,64,64]{1,2,3,0:T(8,128)}, s32[4,64]{1,0:T(4,128)S(1)}, f32[256,64,64]{2,1,0:T(8,128)}, ...), condition=%wide.region_1.2_spmd, body=%wide.region_0.1_spmd.sunk | while | flops 201327808 | bytes 6330441 | solution.py:26
  227.7 4.1 gather_fusion
  231.8 4.7 %fusion.46 = f32[4,64,64]{2,1,0:T(8,128)S(1)} fusion(f32[4,64,64]{2,1,0:T(8,128)S(1)} %get-tuple-element.172, s32[]{:T(128)} %get-tuple-element.171, f32[64,64,64]{2,1,0:T(8,128)S(1)} %gather_fusion, f32[4,64,64,64]{1,2,3,0:T(8,128)} %get-tuple-element.179), kind=kOutput, calls=%fused_computation.7.clone.1 | convolution fusion | flops 201326592 | bytes 4228096 | tf_op jit(solution)/shard_map/while/body/eval_jaxpr/kij,kjf->if/dot_general | solution.py:24
  236.5 4.1 gather_fusion
  240.6 4.7 %fusion.46 = f32[4,64,64]{2,1,0:T(8,128)S(1)} fusion(f32[4,64,64]{2,1,0:T(8,128)S(1)} %get-tuple-element.172, s32[]{:T(128)} %get-tuple-element.171, f32[64,64,64]{2,1,0:T(8,128)S(1)} %gather_fusion, f32[4,64,64,64]{1,2,3,0:T(8,128)} %get-tuple-element.179), kind=kOutput, calls=%fused_computation.7.clone.1 | convolution fusion | flops 201326592 | bytes 4228096 | tf_op jit(solution)/shard_map/while/body/eval_jaxpr/kij,kjf->if/dot_general | solution.py:24
  245.3 4.1 gather_fusion
  249.4 4.7 %fusion.46 = f32[4,64,64]{2,1,0:T(8,128)S(1)} fusion(f32[4,64,64]{2,1,0:T(8,128)S(1)} %get-tuple-element.172, s32[]{:T(128)} %get-tuple-element.171, f32[64,64,64]{2,1,0:T(8,128)S(1)} %gather_fusion, f32[4,64,64,64]{1,2,3,0:T(8,128)} %get-tuple-element.179), kind=kOutput, calls=%fused_computation.7.clone.1 | convolution fusion | flops 201326592 | bytes 4228096 | tf_op jit(solution)/shard_map/while/body/eval_jaxpr/kij,kjf->if/dot_general | solution.py:24
  254.1 4.1 gather_fusion
  258.2 4.7 %fusion.46 = f32[4,64,64]{2,1,0:T(8,128)S(1)} fusion(f32[4,64,64]{2,1,0:T(8,128)S(1)} %get-tuple-element.172, s32[]{:T(128)} %get-tuple-element.171, f32[64,64,64]{2,1,0:T(8,128)S(1)} %gather_fusion, f32[4,64,64,64]{1,2,3,0:T(8,128)} %get-tuple-element.179), kind=kOutput, calls=%fused_computation.7.clone.1 | convolution fusion | flops 201326592 | bytes 4228096 | tf_op jit(solution)/shard_map/while/body/eval_jaxpr/kij,kjf->if/dot_general | solution.py:24
  262.9 0.7 copy.30
  263.6 0.0 all-gather.9.cloned.1.call-update
  263.6 154.2 %all-gather.9.cloned.1.call-done = f32[16384,64]{0,1:T(8,128)} async-done(((f32[256,64]{0,1:T(8,128)}), f32[16384,64]{0,1:T(8,128)}) %all-gather.9.cloned.1.call-update) | async-done | bytes 4194320 | tf_op jit(solution)/shard_map/all_gather | solution.py:38
  417.8 6.9 %copy.31 = f32[16384,64]{1,0:T(8,128)} copy(f32[16384,64]{0,1:T(8,128)} %all-gather.9.cloned.1.call-done) | data formatting | bytes 8388608 | tf_op jit(solution)/shard_map/while | solution.py:26
  424.7 35.2 %while.21 = (s32[]{:T(128)}, f32[4,64,64]{2,1,0:T(8,128)S(1)}, f32[4,64,64,64]{1,2,3,0:T(8,128)}, s32[4,64]{1,0:T(4,128)S(1)}, f32[256,64,64]{2,1,0:T(8,128)}, /*index=5*/s32[]{:T(128)}) while((s32[]{:T(128)}, f32[4,64,64]{2,1,0:T(8,128)S(1)}, f32[4,64,64,64]{1,2,3,0:T(8,128)}, s32[4,64]{1,0:T(4,128)S(1)}, f32[256,64,64]{2,1,0:T(8,128)}, ...), condition=%wide.region_3.4_spmd, body=%wide.region_2.3_spmd.sunk | while | flops 201327808 | bytes 6330441 | solution.py:26
  424.7 4.1 gather_fusion.1
  428.8 4.7 %fusion.50 = f32[4,64,64]{2,1,0:T(8,128)S(1)} fusion(f32[4,64,64]{2,1,0:T(8,128)S(1)} %get-tuple-element.190, s32[]{:T(128)} %get-tuple-element.189, f32[64,64,64]{2,1,0:T(8,128)S(1)} %gather_fusion.1, f32[4,64,64,64]{1,2,3,0:T(8,128)} %get-tuple-element.197), kind=kOutput, calls=%fused_computation.19.clone.1 | convolution fusion | flops 201326592 | bytes 4228096 | tf_op jit(solution)/shard_map/while/body/eval_jaxpr/kij,kjf->if/dot_general | solution.py:24
  433.5 4.1 gather_fusion.1
  437.6 4.7 %fusion.50 = f32[4,64,64]{2,1,0:T(8,128)S(1)} fusion(f32[4,64,64]{2,1,0:T(8,128)S(1)} %get-tuple-element.190, s32[]{:T(128)} %get-tuple-element.189, f32[64,64,64]{2,1,0:T(8,128)S(1)} %gather_fusion.1, f32[4,64,64,64]{1,2,3,0:T(8,128)} %get-tuple-element.197), kind=kOutput, calls=%fused_computation.19.clone.1 | convolution fusion | flops 201326592 | bytes 4228096 | tf_op jit(solution)/shard_map/while/body/eval_jaxpr/kij,kjf->if/dot_general | solution.py:24
  442.3 4.1 gather_fusion.1
  446.4 4.7 %fusion.50 = f32[4,64,64]{2,1,0:T(8,128)S(1)} fusion(f32[4,64,64]{2,1,0:T(8,128)S(1)} %get-tuple-element.190, s32[]{:T(128)} %get-tuple-element.189, f32[64,64,64]{2,1,0:T(8,128)S(1)} %gather_fusion.1, f32[4,64,64,64]{1,2,3,0:T(8,128)} %get-tuple-element.197), kind=kOutput, calls=%fused_computation.19.clone.1 | convolution fusion | flops 201326592 | bytes 4228096 | tf_op jit(solution)/shard_map/while/body/eval_jaxpr/kij,kjf->if/dot_general | solution.py:24
  451.1 4.1 gather_fusion.1
  455.2 4.7 %fusion.50 = f32[4,64,64]{2,1,0:T(8,128)S(1)} fusion(f32[4,64,64]{2,1,0:T(8,128)S(1)} %get-tuple-element.190, s32[]{:T(128)} %get-tuple-element.189, f32[64,64,64]{2,1,0:T(8,128)S(1)} %gather_fusion.1, f32[4,64,64,64]{1,2,3,0:T(8,128)} %get-tuple-element.197), kind=kOutput, calls=%fused_computation.19.clone.1 | convolution fusion | flops 201326592 | bytes 4228096 | tf_op jit(solution)/shard_map/while/body/eval_jaxpr/kij,kjf->if/dot_general | solution.py:24
  459.8 0.7 copy.32
  (19 shorter events, 0.1 us)
Async XLA Ops:
  7.2 49.4 %all-gather.5.cloned.1.call-start = ((), (), s32[]{:S(2)}) async-start(), calls=%async_computation | async-start | bytes 2359296 | tf_op jit(solution)/shard_map/all_gather | solution.py:32
  7.9 212.9 %all-gather.7.cloned.1.call-start = ((), (), s32[]{:S(2)}) async-start(), calls=%async_computation.1 | async-start | bytes 4259840 | tf_op jit(solution)/shard_map/all_gather | solution.py:36
  8.6 409.1 %all-gather.9.cloned.1.call-start = ((), (), s32[]{:S(2)}) async-start(), calls=%async_computation.2 | async-start | bytes 4259840 | tf_op jit(solution)/shard_map/all_gather | solution.py:38
Sparse Core Ops, SparseCore 0:
  10.1 46.4 all-gather.4
  60.9 159.8 all-gather.6
  263.7 154.0 all-gather.8
where the time goes:
time: 468 us; the launch traced here: 467 us
  waiting for transfers between devices  328 us (70%)
  local copies, waits for them, and re-layouts  63.7 us (14%)
  matrix products  37.5 us (8%)
  blocking collectives  15.2 us (3%)
  between operations  13.8 us (3%)
  other arithmetic  8.08 us (2%)
    all_gather x1, waiting for transfers between devices, local(): second_slab = lax.all_gather(hop_one, 'row', axis=0, tiled=True)  154 us
    all_gather x1, waiting for transfers between devices, local(): slab = lax.all_gather(features, 'row', axis=0, tiled=True)  141 us
    dot_general x8, matrix products, single(): jnp.einsum('kij,kjf->if', weight_set, picked, precision=lax.Precision.HIG...  37.5 us
    gather x8, local copies, waits for them, and re-layouts, single(): picked = blocks[col_ids]  32.5 us
    all_gather x1, waiting for transfers between devices, local(): lax.all_gather(adj_values, 'col', axis=1, tiled=True)  31.9 us
    while x2, local copies, waits for them, and re-layouts, propagate(): result = lax.map(single, (weights, col_all))  15.9 us
    all_gather x1, blocking collectives, local(): lax.all_gather(adj_cols, 'col', axis=1, tiled=True)  15.2 us
  transfers between devices with their start and end apart: 3, of which 3 were waited for; matrix products, arithmetic and copies ran while one was open for 5% of the time, Pallas kernels for 0%

commit v1 on v0

--- a/solution.py
+++ b/solution.py
@@ -4,6 +4,9 @@
 from jax.sharding import PartitionSpec as P
 
 BLK = 64
+tell_group = lambda in_array: jnp.concatenate(
+    jax.lax.all_to_all(jnp.stack([in_array] * jax.lax.axis_size("col")), "col", 0, 0), 1
+)
 
 
 def masked_tiles(tile_all, adj_count):
@@ -29,7 +32,7 @@
 
 def local(features, adj_values, adj_cols, adj_count):
     tile_all, col_all = (
-        lax.all_gather(adj_values, "col", axis=1, tiled=True),
+        tell_group(adj_values),
         lax.all_gather(adj_cols, "col", axis=1, tiled=True),
     )
     weights = masked_tiles(tile_all, adj_count)

time: 468 us -> 425 us (0.908)
  waiting for transfers between devices: 328 us -> 232 us
  blocking collectives: 15.2 us -> 55.8 us
  starting transfers between devices: 0.11 us -> 7.47 us
  local copies, waits for them, and re-layouts: 63.7 us -> 69.3 us
    all_gather x1, waiting for transfers between devices: 141 us -> 76.9 us  [local(): slab = lax.all_gather(features, 'row', axis=0, tiled=True)]
    all_gather x1, blocking collectives: 15.2 us -> 55.8 us  [local(): lax.all_gather(adj_cols, 'col', axis=1, tiled=True)]
    all_gather x1 -> x0, waiting for transfers between devices: 31.9 us -> none  [local(): lax.all_gather(adj_values, 'col', axis=1, tiled=True)]
    convert_element_type x0 -> x2, local copies, waits for them, and re-layouts: none -> 10.1 us  [masked_tiles(): tile_all.astype(jnp.float32)]
    all_to_all x0 -> x1, starting transfers between devices: none -> 7.4 us  [jax.lax.all_to_all(jnp.stack([in_array] * jax.lax.axis_size('col')), 'col...]
    reshape x1 -> x0, local copies, waits for them, and re-layouts: 7 us -> none  [masked_tiles(): tile_all.astype(jnp.float32)]
  transfers between devices with their start and end apart: 3 -> 3, of which waited for: 3 -> 2; matrix products, arithmetic and copies ran while one was open for 5% -> 7% of each run, Pallas kernels for 0% -> 0%
where the time goes in v1:
time: 425 us; the launch traced here: 424 us
  waiting for transfers between devices  232 us (55%)
  local copies, waits for them, and re-layouts  69.3 us (16%)
  blocking collectives  55.8 us (13%)
  matrix products  37.5 us (9%)
  between operations  14.1 us (3%)
  other arithmetic  7.95 us (2%)
  starting transfers between devices  7.47 us (2%)
    all_gather x1, waiting for transfers between devices, local(): second_slab = lax.all_gather(hop_one, 'row', axis=0, tiled=True)  154 us
    all_gather x1, waiting for transfers between devices, local(): slab = lax.all_gather(features, 'row', axis=0, tiled=True)  76.9 us
    all_gather x1, blocking collectives, local(): lax.all_gather(adj_cols, 'col', axis=1, tiled=True)  55.8 us
    dot_general x8, matrix products, single(): jnp.einsum('kij,kjf->if', weight_set, picked, precision=lax.Precision.HIG...  37.5 us
    gather x8, local copies, waits for them, and re-layouts, single(): picked = blocks[col_ids]  32.5 us
    while x2, local copies, waits for them, and re-layouts, propagate(): result = lax.map(single, (weights, col_all))  15.8 us
    convert_element_type x2, local copies, waits for them, and re-layouts, masked_tiles(): tile_all.astype(jnp.float32)  10.1 us
  transfers between devices with their start and end apart: 3, of which 2 were waited for; matrix products, arithmetic and copies ran while one was open for 7% of the time, Pallas kernels for 0%

profile of v1, /device:TPU:2, one launch (start us, length us, event | category | flops | bytes accessed | tf_op | source)
XLA Modules:
  0.0 424.1 jit_solution(17703573662531840142)
XLA Ops:
  7.2 0.0 all-gather.4.cloned.1.call-start
  7.2 0.7 all-gather.4.cloned.1.call-update
  7.9 2.5 stack.2
  10.4 0.0 copy-start
  10.4 0.0 copy-start.1
  10.4 7.4 %all-to-all-start = ((bf16[8,4,8,4096]{3,2,1,0:T(8,128)(2,1)}), bf16[8,4,8,4096]{3,2,1,0:T(8,128)(2,1)S(1)}, u32[]{:S(2)}, u32[]{:S(2)}) async-start(bf16[8,4,8,4096]{3,2,1,0:T(8,128)(2,1)} %stack.2), calls=%async_computation | async-start | bytes 4194304 | tf_op jit(solution)/shard_map/all_to_all | solution.py:8
  17.8 0.0 all-gather.6.cloned.1.call-start
  17.9 0.0 copy-done
  17.9 55.8 %all-gather = s32[8,8,4]{1,2,0:T(4,128)S(1)} all-gather(s32[1,8,4]{1,2,0:T(4,128)S(1)} %bitcast.74), channel_id=1, replica_groups=mesh['row'=64,'col'=8] {'col'}, dimensions={0}, use_global_device_ids=true | all-gather | bytes 1152 | tf_op jit(solution)/shard_map/all_gather | solution.py:36
  73.7 0.1 reshape.124
  73.7 0.0 copy-done.1
  73.7 0.1 fusion.34
  73.8 0.0 all-to-all-done
  73.8 0.5 convert_bitcast_fusion
  74.3 2.2 copy.23
  76.6 7.8 %reshape.106 = f32[4,64,64,64]{3,2,1,0:T(8,128)} reshape(f32[4,8,8,4096]{3,2,1,0:T(8,128)} %copy.23) | data formatting | bytes 8388608 | tf_op jit(solution)/shard_map/convert_element_type | solution.py:16
  84.4 7.3 %broadcast_multiply_fusion = f32[4,64,64,64]{3,2,1,0:T(8,128)} fusion(f32[4,64,64,64]{3,2,1,0:T(8,128)} %reshape.106, f32[4,64]{1,0:T(4,128)S(1)} %fusion.34), kind=kLoop, calls=%fused_computation.27 | loop fusion | flops 1048576 | bytes 8389632 | tf_op jit(solution)/shard_map/mul | solution.py:17
  91.7 9.0 %copy.26 = f32[4,64,64,64]{1,2,3,0:T(8,128)} copy(f32[4,64,64,64]{3,2,1,0:T(8,128)} %broadcast_multiply_fusion) | data formatting | bytes 8388608 | tf_op jit(solution)/shard_map/while | solution.py:29
  100.7 76.9 %all-gather.4.cloned.1.call-done = f32[16384,64]{0,1:T(8,128)} async-done(((f32[256,64]{0,1:T(8,128)}), f32[16384,64]{0,1:T(8,128)}) %all-gather.4.cloned.1.call-update) | async-done | bytes 4194320 | tf_op jit(solution)/shard_map/all_gather | solution.py:39
  177.5 6.8 %copy.25 = f32[16384,64]{1,0:T(8,128)} copy(f32[16384,64]{0,1:T(8,128)} %all-gather.4.cloned.1.call-done) | data formatting | bytes 8388608 | tf_op jit(solution)/shard_map/all_gather | solution.py:39
  184.4 35.2 %while.20 = (s32[]{:T(128)}, f32[4,64,64]{2,1,0:T(8,128)S(1)}, f32[4,64,64,64]{1,2,3,0:T(8,128)}, s32[4,64]{1,0:T(4,128)S(1)}, f32[256,64,64]{2,1,0:T(8,128)}, /*index=5*/s32[]{:T(128)}) while((s32[]{:T(128)}, f32[4,64,64]{2,1,0:T(8,128)S(1)}, f32[4,64,64,64]{1,2,3,0:T(8,128)}, s32[4,64]{1,0:T(4,128)S(1)}, f32[256,64,64]{2,1,0:T(8,128)}, ...), condition=%wide.region_1.2_spmd, body=%wide.region_0.1_spmd.sunk | while | flops 201327808 | bytes 6330441 | solution.py:29
  184.4 4.1 gather_fusion
  188.5 4.7 %fusion.46 = f32[4,64,64]{2,1,0:T(8,128)S(1)} fusion(f32[4,64,64]{2,1,0:T(8,128)S(1)} %get-tuple-element.172, s32[]{:T(128)} %get-tuple-element.171, f32[64,64,64]{2,1,0:T(8,128)S(1)} %gather_fusion, f32[4,64,64,64]{1,2,3,0:T(8,128)} %get-tuple-element.179), kind=kOutput, calls=%fused_computation.7.clone.1 | convolution fusion | flops 201326592 | bytes 4228096 | tf_op jit(solution)/shard_map/while/body/eval_jaxpr/kij,kjf->if/dot_general | solution.py:27
  193.2 4.1 gather_fusion
  197.3 4.7 %fusion.46 = f32[4,64,64]{2,1,0:T(8,128)S(1)} fusion(f32[4,64,64]{2,1,0:T(8,128)S(1)} %get-tuple-element.172, s32[]{:T(128)} %get-tuple-element.171, f32[64,64,64]{2,1,0:T(8,128)S(1)} %gather_fusion, f32[4,64,64,64]{1,2,3,0:T(8,128)} %get-tuple-element.179), kind=kOutput, calls=%fused_computation.7.clone.1 | convolution fusion | flops 201326592 | bytes 4228096 | tf_op jit(solution)/shard_map/while/body/eval_jaxpr/kij,kjf->if/dot_general | solution.py:27
  202.0 4.1 gather_fusion
  206.1 4.7 %fusion.46 = f32[4,64,64]{2,1,0:T(8,128)S(1)} fusion(f32[4,64,64]{2,1,0:T(8,128)S(1)} %get-tuple-element.172, s32[]{:T(128)} %get-tuple-element.171, f32[64,64,64]{2,1,0:T(8,128)S(1)} %gather_fusion, f32[4,64,64,64]{1,2,3,0:T(8,128)} %get-tuple-element.179), kind=kOutput, calls=%fused_computation.7.clone.1 | convolution fusion | flops 201326592 | bytes 4228096 | tf_op jit(solution)/shard_map/while/body/eval_jaxpr/kij,kjf->if/dot_general | solution.py:27
  210.8 4.1 gather_fusion
  214.9 4.7 %fusion.46 = f32[4,64,64]{2,1,0:T(8,128)S(1)} fusion(f32[4,64,64]{2,1,0:T(8,128)S(1)} %get-tuple-element.172, s32[]{:T(128)} %get-tuple-element.171, f32[64,64,64]{2,1,0:T(8,128)S(1)} %gather_fusion, f32[4,64,64,64]{1,2,3,0:T(8,128)} %get-tuple-element.179), kind=kOutput, calls=%fused_computation.7.clone.1 | convolution fusion | flops 201326592 | bytes 4228096 | tf_op jit(solution)/shard_map/while/body/eval_jaxpr/kij,kjf->if/dot_general | solution.py:27
  219.6 0.7 copy.31
  220.3 0.0 all-gather.6.cloned.1.call-update
  220.3 154.2 %all-gather.6.cloned.1.call-done = f32[16384,64]{0,1:T(8,128)} async-done(((f32[256,64]{0,1:T(8,128)}), f32[16384,64]{0,1:T(8,128)}) %all-gather.6.cloned.1.call-update) | async-done | bytes 4194320 | tf_op jit(solution)/shard_map/all_gather | solution.py:41
  374.5 6.8 %copy.32 = f32[16384,64]{1,0:T(8,128)} copy(f32[16384,64]{0,1:T(8,128)} %all-gather.6.cloned.1.call-done) | data formatting | bytes 8388608 | tf_op jit(solution)/shard_map/while | solution.py:29
  381.4 35.2 %while.21 = (s32[]{:T(128)}, f32[4,64,64]{2,1,0:T(8,128)S(1)}, f32[4,64,64,64]{1,2,3,0:T(8,128)}, s32[4,64]{1,0:T(4,128)S(1)}, f32[256,64,64]{2,1,0:T(8,128)}, /*index=5*/s32[]{:T(128)}) while((s32[]{:T(128)}, f32[4,64,64]{2,1,0:T(8,128)S(1)}, f32[4,64,64,64]{1,2,3,0:T(8,128)}, s32[4,64]{1,0:T(4,128)S(1)}, f32[256,64,64]{2,1,0:T(8,128)}, ...), condition=%wide.region_3.4_spmd, body=%wide.region_2.3_spmd.sunk | while | flops 201327808 | bytes 6330441 | solution.py:29
  381.4 4.1 gather_fusion.1
  385.5 4.7 %fusion.50 = f32[4,64,64]{2,1,0:T(8,128)S(1)} fusion(f32[4,64,64]{2,1,0:T(8,128)S(1)} %get-tuple-element.190, s32[]{:T(128)} %get-tuple-element.189, f32[64,64,64]{2,1,0:T(8,128)S(1)} %gather_fusion.1, f32[4,64,64,64]{1,2,3,0:T(8,128)} %get-tuple-element.197), kind=kOutput, calls=%fused_computation.19.clone.1 | convolution fusion | flops 201326592 | bytes 4228096 | tf_op jit(solution)/shard_map/while/body/eval_jaxpr/kij,kjf->if/dot_general | solution.py:27
  390.2 4.1 gather_fusion.1
  394.3 4.7 %fusion.50 = f32[4,64,64]{2,1,0:T(8,128)S(1)} fusion(f32[4,64,64]{2,1,0:T(8,128)S(1)} %get-tuple-element.190, s32[]{:T(128)} %get-tuple-element.189, f32[64,64,64]{2,1,0:T(8,128)S(1)} %gather_fusion.1, f32[4,64,64,64]{1,2,3,0:T(8,128)} %get-tuple-element.197), kind=kOutput, calls=%fused_computation.19.clone.1 | convolution fusion | flops 201326592 | bytes 4228096 | tf_op jit(solution)/shard_map/while/body/eval_jaxpr/kij,kjf->if/dot_general | solution.py:27
  399.0 4.1 gather_fusion.1
  403.1 4.7 %fusion.50 = f32[4,64,64]{2,1,0:T(8,128)S(1)} fusion(f32[4,64,64]{2,1,0:T(8,128)S(1)} %get-tuple-element.190, s32[]{:T(128)} %get-tuple-element.189, f32[64,64,64]{2,1,0:T(8,128)S(1)} %gather_fusion.1, f32[4,64,64,64]{1,2,3,0:T(8,128)} %get-tuple-element.197), kind=kOutput, calls=%fused_computation.19.clone.1 | convolution fusion | flops 201326592 | bytes 4228096 | tf_op jit(solution)/shard_map/while/body/eval_jaxpr/kij,kjf->if/dot_general | solution.py:27
  407.8 4.1 gather_fusion.1
  411.9 4.7 %fusion.50 = f32[4,64,64]{2,1,0:T(8,128)S(1)} fusion(f32[4,64,64]{2,1,0:T(8,128)S(1)} %get-tuple-element.190, s32[]{:T(128)} %get-tuple-element.189, f32[64,64,64]{2,1,0:T(8,128)S(1)} %gather_fusion.1, f32[4,64,64,64]{1,2,3,0:T(8,128)} %get-tuple-element.197), kind=kOutput, calls=%fused_computation.19.clone.1 | convolution fusion | flops 201326592 | bytes 4228096 | tf_op jit(solution)/shard_map/while/body/eval_jaxpr/kij,kjf->if/dot_general | solution.py:27
  416.6 0.7 copy.33
  (19 shorter events, 0.1 us)
Async XLA Ops:
  7.2 170.4 %all-gather.4.cloned.1.call-start = ((), (), s32[]{:S(2)}) async-start(), calls=%async_computation.1 | async-start | bytes 4259840 | tf_op jit(solution)/shard_map/all_gather | solution.py:39
  10.4 7.4 %copy-start = (s32[4,8]{1,0:T(4,128)S(1)}, s32[4,8]{1,0:T(4,128)}, u32[]{:S(2)}) copy-start(s32[4,8]{1,0:T(4,128)} %param.10) | copy-start | bytes 388
  10.4 63.3 %copy-start.1 = (s32[4]{0:T(128)S(1)}, s32[4]{0:T(128)}, u32[]{:S(2)}) copy-start(s32[4]{0:T(128)} %param.11) | copy-start | bytes 52
  10.4 63.4 %all-to-all-start = ((bf16[8,4,8,4096]{3,2,1,0:T(8,128)(2,1)}), bf16[8,4,8,4096]{3,2,1,0:T(8,128)(2,1)S(1)}, u32[]{:S(2)}, u32[]{:S(2)}) async-start(bf16[8,4,8,4096]{3,2,1,0:T(8,128)(2,1)} %stack.2), calls=%async_computation | async-start | bytes 4194304 | tf_op jit(solution)/shard_map/all_to_all | solution.py:8
  17.8 356.7 %all-gather.6.cloned.1.call-start = ((), (), s32[]{:S(2)}) async-start(), calls=%async_computation.2 | async-start | bytes 4259840 | tf_op jit(solution)/shard_map/all_gather | solution.py:41
Sparse Core Ops, SparseCore 0:
  12.3 165.1 all-gather.3
  220.4 154.0 all-gather.5
